TPU v7x, 32 devices: a whole 2x2x4 slice. The times are simulated.
32 devices in a mesh: dp: 8 (over y, x, core), mp: 4 (over z).
Axes of the slice: x: 2, y: 2, z: 4, core: 2. Of those that a mesh axis runs over, the one named last changes fastest.
Arguments:
- token_ids: int32 [8, 1024], P('dp'), may hold values from 0 to 50303
- prompt_len: int32 [8], replicated, may hold values from 1 to 512, as said below
- example_len: int32 [8], replicated, may hold values from 512 to 1024, as said below
- embedding: bfloat16 [50304, 1024], P('mp'), may hold values from -6 to 6
- w_qkv: bfloat16 [1024, 3072], P(None, 'mp'), may hold values from -0.1875 to 0.1875
- w_out: bfloat16 [1024, 1024], P('mp'), may hold values from -0.75 to 0.75
- w_in: bfloat16 [1024, 4096], P(None, 'mp'), may hold values from -0.1875 to 0.1875
- b_in: float32 [4096], P('mp'), may hold values from -3 to 3
- w_down: bfloat16 [4096, 1024], P('mp'), may hold values from -0.09375 to 0.09375
- unembed: bfloat16 [1024, 50304], P('dp', 'mp'), may hold values from -0.1875 to 0.1875
- ln_gain: float32 [3, 1024], replicated, may hold values from 0.5 to 1.5
- ln_bias: float32 [3, 1024], replicated, may hold values from -3 to 3
- master: float32 [8, 1024, 128], P(None, ('dp', 'mp')), may hold values from -0.1875 to 0.1875
- first_moment: float32 [8, 1024, 128], P(None, ('dp', 'mp')), may hold values from -1.5258789e-05 to 1.5258789e-05
- second_moment: float32 [8, 1024, 128], P(None, ('dp', 'mp')), may hold values from 4.7683716e-14 to 7.6293946e-13
- eigen_bases: float32 [8, 128, 128], replicated, as said below
Outputs:
- mean_loss: float32 [], replicated
- grad_norm: float32 [], replicated
- new_first: float32 [8, 1024, 128], P(None, ('dp', 'mp'))
- new_second: float32 [8, 1024, 128], P(None, ('dp', 'mp'))
- new_master: float32 [8, 1024, 128], P(None, ('dp', 'mp'))
Inputs may be any that keep to these rules, and one draw needn't show every extreme that they name: `prompt_len`: each at most half of its example's length; the first example's is 512. `example_len`: the first example is 1024 tokens long. `eigen_bases`: each matrix is orthogonal.
All inputs are finite; a program needn't handle non-finite values.
Results may differ from a plain program's by a relative error of at most 0.0024.
Values may be sent and summed in bfloat16 or wider, within the bound.
A program may use at most 192 MiB of HBM per device.

v0:
```python
import jax
import jax.numpy as jnp
from jax import lax
from jax.sharding import PartitionSpec as P

D = 1024
HEADS = 16
R = 128
ADAM_STEP = 10
HD = 64
ROT = 16
HIGH_PRECISION = lax.Precision.HIGHEST
NORM_EPS = 1e-05
ROPE_BASE = 10000.0
CLIP_LIMIT = 0.01
LEARN_RATE = 0.02
BETA_FIRST = 0.9
BETA_SECOND = 0.999
ADAM_EPS = 1e-08
DECAY_RATE = 0.01


def merged(value, axis, join):
    pieces = jax.tree.map(lambda part: lax.all_gather(part, axis), value)
    head = jax.tree.map(lambda part: part[0], pieces)
    tail = jax.tree.map(lambda part: part[1:], pieces)
    running, _ = lax.scan(lambda running, section: (join(running, section), None), head, tail)
    return running


def layer_norm(values, gain, shift):
    centre = values - jnp.mean(values, -1, keepdims=True)
    spread = jnp.mean(centre * centre, -1, keepdims=True)
    return centre * lax.rsqrt(spread + NORM_EPS) * gain + shift


def norm_back(values, gain, shift, upstream):
    _, pullback = jax.vjp(lambda inputs: layer_norm(inputs, gain, shift), values)
    return pullback(upstream)[0]


def rope_tables(length):
    half = ROT // 2
    freqs = ROPE_BASE ** (-2.0 * jnp.arange(half, dtype=jnp.float32) / ROT)
    angles = jnp.arange(length, dtype=jnp.float32)[:, None] * freqs[None, :]
    return (jnp.cos(angles)[:, None, :], jnp.sin(angles)[:, None, :])


def rotate(field, cosine, sine):
    half = ROT // 2
    first = field[..., :half]
    second = field[..., half:ROT]
    return jnp.concatenate(
        [first * cosine - second * sine, second * cosine + first * sine, field[..., ROT:]], -1
    )


def rotate_back(upstream, cosine, sine):
    half = ROT // 2
    first = upstream[..., :half]
    second = upstream[..., half:ROT]
    return jnp.concatenate(
        [first * cosine + second * sine, second * cosine - first * sine, upstream[..., ROT:]], -1
    )


def masked_scores(queries, key_rows, start_row, stop_row):
    scores = jnp.einsum(
        "qhd,khd->hqk",
        queries[start_row:stop_row],
        key_rows[:stop_row],
        preferred_element_type=jnp.float32,
    ) * HD ** (-0.5)
    query_pos = start_row + jnp.arange(stop_row - start_row)[:, None]
    causal = jnp.arange(stop_row)[None, :] <= query_pos
    return jnp.where(causal[None], scores, -1e30)


def attend(queries, key_rows, value_rows):
    length = queries.shape[0]
    row_block = min(512, length)
    outputs = []
    spreads = []
    for start_row in range(0, length, row_block):
        stop_row = start_row + row_block
        scores = masked_scores(queries, key_rows, start_row, stop_row)
        top_score = jnp.max(scores, -1, keepdims=True)
        weights = jnp.exp(scores - top_score)
        row_total = jnp.sum(weights, -1, keepdims=True)
        probs = (weights / row_total).astype(jnp.bfloat16)
        outputs.append(
            jnp.einsum(
                "hqk,khd->qhd", probs, value_rows[:stop_row], preferred_element_type=jnp.float32
            )
        )
        spreads.append((top_score + jnp.log(row_total))[..., 0])
    return (jnp.concatenate(outputs, 0).astype(jnp.bfloat16), jnp.concatenate(spreads, 1))


def attend_back(queries, key_rows, value_rows, spreads, upstream):
    length = queries.shape[0]
    row_block = min(512, length)
    scaling = HD ** (-0.5)
    query_grads = []
    key_grad = jnp.zeros(key_rows.shape, jnp.float32)
    value_grad = jnp.zeros(value_rows.shape, jnp.float32)
    for start_row in range(0, length, row_block):
        stop_row = start_row + row_block
        scores = masked_scores(queries, key_rows, start_row, stop_row)
        probs = jnp.exp(scores - spreads[:, start_row:stop_row, None])
        grad_here = upstream[start_row:stop_row]
        prob_grad = jnp.einsum(
            "qhd,khd->hqk", grad_here, value_rows[:stop_row], preferred_element_type=jnp.float32
        )
        inner_sum = jnp.sum(probs * prob_grad, -1, keepdims=True)
        score_grad = (probs * (prob_grad - inner_sum)).astype(jnp.bfloat16)
        query_grads.append(
            jnp.einsum(
                "hqk,khd->qhd", score_grad, key_rows[:stop_row], preferred_element_type=jnp.float32
            )
            * scaling
        )
        key_grad = key_grad.at[:stop_row].add(
            jnp.einsum(
                "hqk,qhd->khd",
                score_grad,
                queries[start_row:stop_row],
                preferred_element_type=jnp.float32,
            )
            * scaling
        )
        value_grad = value_grad.at[:stop_row].add(
            jnp.einsum(
                "hqk,qhd->khd",
                probs.astype(jnp.bfloat16),
                grad_here,
                preferred_element_type=jnp.float32,
            )
        )
    return (jnp.concatenate(query_grads, 0), key_grad, value_grad)


def merge_stats(first, second):
    top_score = jnp.maximum(first[0], second[0])
    row_total = first[1] * jnp.exp(first[0] - top_score) + second[1] * jnp.exp(
        second[0] - top_score
    )
    return (top_score, row_total, first[2] + second[2])


def per_device(
    token_ids,
    prompt_len,
    example_len,
    embedding,
    w_qkv,
    w_out,
    w_in,
    b_in,
    w_down,
    unembed,
    ln_gain,
    ln_bias,
    master,
    first_moment,
    second_moment,
    eigen_bases,
):
    group_count = lax.axis_size("mp")
    group_index = lax.axis_index("mp")
    adapters = lax.all_gather(master.astype(jnp.bfloat16), ("dp", "mp"), axis=1, tiled=True)
    head_local = lax.all_gather(unembed, "dp", axis=0, tiled=True)
    examples, length = token_ids.shape
    width = embedding.shape[0]
    vocab_local = head_local.shape[1]
    rows = examples * length
    local_heads = HEADS // group_count
    group_width = local_heads * HD
    flat_ids = token_ids.reshape(rows)
    relative = flat_ids - group_index * width
    inside = (relative >= 0) & (relative < width)
    picked = jnp.where(
        inside[:, None], embedding[jnp.clip(relative, 0, width - 1)].astype(jnp.float32), 0.0
    )
    start_rows = lax.psum(picked.astype(jnp.bfloat16), "mp").astype(jnp.float32)
    leading_example = lax.axis_index("dp") * examples
    prompts = lax.dynamic_slice_in_dim(prompt_len, leading_example, examples)
    totals = lax.dynamic_slice_in_dim(example_len, leading_example, examples)
    position = jnp.arange(length)
    keep = (position[None, :] >= prompts[:, None] - 1) & (position[None, :] < totals[:, None] - 1)
    count = jnp.sum(example_len - prompt_len).astype(jnp.float32)
    row_weight = keep.reshape(rows).astype(jnp.float32) / count
    target = jnp.roll(token_ids, -1, axis=1).reshape(rows)
    normed_attn = layer_norm(start_rows, ln_gain[0], ln_bias[0]).astype(jnp.bfloat16)
    normed_ffn = layer_norm(start_rows, ln_gain[1], ln_bias[1]).astype(jnp.bfloat16)
    inner = jnp.dot(
        normed_attn,
        jnp.concatenate([adapters[0], adapters[1], adapters[2]], 1),
        preferred_element_type=jnp.float32,
    ).astype(jnp.bfloat16)
    base = jnp.dot(normed_attn, w_qkv, preferred_element_type=jnp.float32).reshape(
        rows, local_heads, 3, HD
    )
    adapter_rows = [
        lax.dynamic_slice_in_dim(
            adapters[3 + selector_index], group_index * group_width, group_width, 0
        )
        for selector_index in range(3)
    ]
    pre_parts = []
    for selector_index in range(3):
        extra = jnp.einsum(
            "lr,dr->ld",
            inner[:, selector_index * R : (selector_index + 1) * R],
            adapter_rows[selector_index],
            preferred_element_type=jnp.float32,
        )
        pre_parts.append(base[:, :, selector_index] + extra.reshape(rows, local_heads, HD))
    cosine, sine = rope_tables(length)
    queries = rotate(pre_parts[0].reshape(examples, length, local_heads, HD), cosine, sine).astype(
        jnp.bfloat16
    )
    key_rows = rotate(pre_parts[1].reshape(examples, length, local_heads, HD), cosine, sine).astype(
        jnp.bfloat16
    )
    value_rows = pre_parts[2].reshape(examples, length, local_heads, HD).astype(jnp.bfloat16)
    sample = 0
    context_here, spread_local = attend(queries[sample], key_rows[sample], value_rows[sample])
    spreads = [spread_local]
    context = context_here.reshape(rows, group_width)
    out_rows = lax.dynamic_slice_in_dim(adapters[6], group_index * group_width, group_width, 0)
    inner_out = jnp.dot(context, out_rows, preferred_element_type=jnp.float32).astype(jnp.bfloat16)
    hidden = jax.nn.gelu(
        jnp.dot(normed_ffn, w_in, preferred_element_type=jnp.float32) + b_in, approximate=False
    ).astype(jnp.bfloat16)
    partial_value = (
        jnp.dot(context, w_out, preferred_element_type=jnp.float32)
        + jnp.einsum("lr,dr->ld", inner_out, adapters[7], preferred_element_type=jnp.float32)
        + jnp.dot(hidden, w_down, preferred_element_type=jnp.float32)
    )
    resid = start_rows + lax.psum(partial_value, "mp")
    final_rows = layer_norm(resid, ln_gain[2], ln_bias[2]).astype(jnp.bfloat16)
    row_block = min(256, rows)
    blocks = rows // row_block
    vocab_ids = jnp.arange(vocab_local)[None, :]

    def block_stats(pieces):
        rows_here, target_here = pieces
        logits = jnp.dot(rows_here, head_local, preferred_element_type=jnp.float32)
        top_score = jnp.max(logits, -1)
        row_total = jnp.sum(jnp.exp(logits - top_score[:, None]), -1)
        hit = vocab_ids == (target_here - group_index * vocab_local)[:, None]
        return (top_score, row_total, jnp.sum(jnp.where(hit, logits, 0.0), -1))

    stats = lax.map(
        block_stats, (final_rows.reshape(blocks, row_block, D), target.reshape(blocks, row_block))
    )
    top_score, row_total, target_logit = merged(
        (stats[0].reshape(rows), stats[1].reshape(rows), stats[2].reshape(rows)), "mp", merge_stats
    )
    spread_all = top_score + jnp.log(row_total)
    local_loss = jnp.sum((spread_all - target_logit) * row_weight)

    def block_back(pieces):
        rows_here, target_here, spread_local, weight_here = pieces
        logits = jnp.dot(rows_here, head_local, preferred_element_type=jnp.float32)
        hit = (vocab_ids == (target_here - group_index * vocab_local)[:, None]).astype(jnp.float32)
        logit_grad = (
            (jnp.exp(logits - spread_local[:, None]) - hit) * weight_here[:, None]
        ).astype(jnp.bfloat16)
        return jnp.einsum("lv,dv->ld", logit_grad, head_local, preferred_element_type=jnp.float32)

    head_grad = lax.map(
        block_back,
        (
            final_rows.reshape(blocks, row_block, D),
            target.reshape(blocks, row_block),
            spread_all.reshape(blocks, row_block),
            row_weight.reshape(blocks, row_block),
        ),
    ).reshape(rows, D)
    branch_grad = norm_back(resid, ln_gain[2], ln_bias[2], lax.psum(head_grad, "mp")).astype(
        jnp.bfloat16
    )
    inner_out_grad = jnp.dot(branch_grad, adapters[7], preferred_element_type=jnp.float32).astype(
        jnp.bfloat16
    )
    grad_out_b = jnp.einsum("ld,lr->dr", branch_grad, inner_out, preferred_element_type=jnp.float32)
    grad_out_a = jnp.einsum(
        "ld,lr->dr", context, inner_out_grad, preferred_element_type=jnp.float32
    )
    context_grad = jnp.einsum(
        "ld,ed->le", branch_grad, w_out, preferred_element_type=jnp.float32
    ) + jnp.einsum("lr,dr->ld", inner_out_grad, out_rows, preferred_element_type=jnp.float32)
    context_grad = context_grad.astype(jnp.bfloat16).reshape(examples, length, local_heads, HD)
    sample = 0
    query_grad, key_grad, value_grad = attend_back(
        queries[sample], key_rows[sample], value_rows[sample], spreads[sample], context_grad[sample]
    )
    query_parts = [rotate_back(query_grad, cosine, sine)]
    key_parts = [rotate_back(key_grad, cosine, sine)]
    value_parts = [value_grad]
    pre_grads = [
        parts[0].reshape(rows, group_width).astype(jnp.bfloat16)
        for parts in (query_parts, key_parts, value_parts)
    ]
    complete_gradients = []
    local_grads = []
    for selector_index in range(3):
        projected_values = jnp.einsum(
            "ld,le->de", normed_attn, pre_grads[selector_index], preferred_element_type=jnp.float32
        )
        complete_gradients.append(
            jnp.dot(
                projected_values,
                adapter_rows[selector_index].astype(jnp.float32),
                precision=HIGH_PRECISION,
            )
        )
        local_grads.append(
            jnp.einsum(
                "ld,lr->dr",
                pre_grads[selector_index],
                inner[:, selector_index * R : (selector_index + 1) * R],
                preferred_element_type=jnp.float32,
            )
        )
    local_grads.append(grad_out_a)
    placed = lax.dynamic_update_slice(
        jnp.zeros((4, D, R), jnp.float32), jnp.stack(local_grads), (0, group_index * group_width, 0)
    )
    gradient = jnp.concatenate([jnp.stack(complete_gradients), placed, grad_out_b[None]], 0)
    owned = lax.psum_scatter(gradient, ("dp", "mp"), scatter_dimension=1, tiled=True)
    squares = jnp.sum(owned * owned)
    norm_squared = lax.psum(squares, ("dp", "mp"))
    mean_loss = lax.psum(local_loss, "dp")
    grad_norm = jnp.sqrt(norm_squared)
    clipped = owned * jnp.minimum(1.0, CLIP_LIMIT / grad_norm)
    rotated = jnp.einsum("mdr,mrs->mds", clipped, eigen_bases, precision=HIGH_PRECISION)
    new_first = BETA_FIRST * first_moment + (1.0 - BETA_FIRST) * rotated
    new_second = BETA_SECOND * second_moment + (1.0 - BETA_SECOND) * rotated * rotated
    normed = (
        new_first
        / (1.0 - BETA_FIRST**ADAM_STEP)
        / (jnp.sqrt(new_second / (1.0 - BETA_SECOND**ADAM_STEP)) + ADAM_EPS)
    )
    turned = jnp.einsum("mds,mrs->mdr", normed, eigen_bases, precision=HIGH_PRECISION)
    new_master = master - LEARN_RATE * (turned + DECAY_RATE * master)
    return (mean_loss, grad_norm, new_first, new_second, new_master)


def solution(mesh):
    placed = (
        P("dp", None),
        P(),
        P(),
        P("mp", None),
        P(None, "mp"),
        P("mp", None),
        P(None, "mp"),
        P("mp"),
        P("mp", None),
        P("dp", "mp"),
        P(),
        P(),
        P(None, ("dp", "mp"), None),
        P(None, ("dp", "mp"), None),
        P(None, ("dp", "mp"), None),
        P(),
    )
    return jax.shard_map(
        per_device,
        mesh=mesh,
        in_specs=placed,
        out_specs=(
            P(),
            P(),
            P(None, ("dp", "mp"), None),
            P(None, ("dp", "mp"), None),
            P(None, ("dp", "mp"), None),
        ),
        check_vma=False,
    )
```

profile of v0, /device:TPU:14, one launch (start us, length us, event | category | flops | bytes accessed | tf_op | source)
XLA Modules:
  0.0 1017.0 jit_solution(3470732560925565724)
XLA Ops:
  9.6 17.7 %gather_fusion = bf16[1024,1024]{1,0:T(8,128)(2,1)} fusion(bf16[12576,1024]{1,0:T(8,128)(2,1)} %param.37, s32[1024]{0:T(1024)S(1)} %broadcast_clamp_fusion), kind=kCustom, calls=%fused_computation | custom fusion | bytes 4198400 | tf_op jit(solution)/shard_map/gather | solution.py:183
  32.3 87.9 %all-reduce.6.cloned.1.call-done = bf16[1024,1024]{1,0:T(8,128)(2,1)} async-done(((bf16[1024,1024]{1,0:T(8,128)(2,1)}), bf16[1024,1024]{1,0:T(8,128)(2,1)}) %all-reduce.6.cloned.1.call-update) | async-done | bytes 2097168 | tf_op jit(solution)/shard_map/psum | solution.py:185
  129.1 16.4 %fusion.56 = f32[1024,1024]{1,0:T(8,128)} fusion(bf16[1024,1024]{1,0:T(8,128)(2,1)S(1)} %copy-done, f32[1024]{0:T(1024)S(1)} %copy-done.75, bf16[1024,1024]{1,0:T(8,128)(2,1)} %param.40, bf16[1024,1024]{1,0:T(8,128)(2,1)} %all-reduce.6.cloned.1.call-done, f32[1024]{0:T(1024)S(1)} %bitcast.338, f32[1024]{0:T(1024)S(1)} %bitcast.337, ...), kind=kOutput, calls=%fused_computation.95 | convolution fusion | flops 4370464768 | bytes 10506240 | tf_op jit(solution)/shard_map/dot_general | solution.py:239
  179.2 142.3 %all-reduce.8.cloned.1.call-done = f32[1024,1024]{1,0:T(8,128)} async-done(((f32[1024,1024]{1,0:T(8,128)}), f32[1024,1024]{1,0:T(8,128)}) %all-reduce.8.cloned.1.call-update) | async-done | bytes 4194320 | tf_op jit(solution)/shard_map/psum | solution.py:241
  328.2 102.9 %while.54 = (s32[]{:T(128)}, f32[4,256]{1,0:T(4,128)S(1)}, f32[4,256]{1,0:T(4,128)S(1)}, f32[4,256]{1,0:T(4,128)S(1)}, bf16[4,256,1024]{2,1,0:T(8,128)(2,1)}, /*...) while((s32[]{:T(128)}, f32[4,256]{1,0:T(4,128)S(1)}, ...), condition=%wide.region_14.15_spmd.clone.clone, body=%wide.region_10.14_spmd.clone.sunk.clone | while | flops 6612762112 | bytes 52246120 | solution.py:255
  328.2 18.8 %fusion.255 = (f32[256]{0:T(256)S(1)}, f32[256,12576]{0,1:T(8,128)}) fusion(bf16[1024,12576]{1,0:T(8,128)(2,1)} %get-tuple-element.709, bf16[4,256,1024]{2,1,0:T(8,128)(2,1)} %get-tuple-element.708, s32[]{:T(128)} %get-tuple-element.696), kind=kOutput, calls=%fused_computation.294.clone.1.clone | convolution fusion | flops 6596665344 | bytes 39355904 | tf_op jit(solution)/shard_map/while/body/eval_jaxpr/dot_general | solution.py:249
  354.0 18.9 %fusion.255 = (f32[256]{0:T(256)S(1)}, f32[256,12576]{0,1:T(8,128)}) fusion(bf16[1024,12576]{1,0:T(8,128)(2,1)} %get-tuple-element.709, bf16[4,256,1024]{2,1,0:T(8,128)(2,1)} %get-tuple-element.708, s32[]{:T(128)} %get-tuple-element.696), kind=kOutput, calls=%fused_computation.294.clone.1.clone | convolution fusion | flops 6596665344 | bytes 39355904 | tf_op jit(solution)/shard_map/while/body/eval_jaxpr/dot_general | solution.py:249
  372.9 6.7 select_reduce_fusion.3
  379.7 18.9 %fusion.255 = (f32[256]{0:T(256)S(1)}, f32[256,12576]{0,1:T(8,128)}) fusion(bf16[1024,12576]{1,0:T(8,128)(2,1)} %get-tuple-element.709, bf16[4,256,1024]{2,1,0:T(8,128)(2,1)} %get-tuple-element.708, s32[]{:T(128)} %get-tuple-element.696), kind=kOutput, calls=%fused_computation.294.clone.1.clone | convolution fusion | flops 6596665344 | bytes 39355904 | tf_op jit(solution)/shard_map/while/body/eval_jaxpr/dot_general | solution.py:249
  398.6 6.7 select_reduce_fusion.3
  405.5 18.8 %fusion.255 = (f32[256]{0:T(256)S(1)}, f32[256,12576]{0,1:T(8,128)}) fusion(bf16[1024,12576]{1,0:T(8,128)(2,1)} %get-tuple-element.709, bf16[4,256,1024]{2,1,0:T(8,128)(2,1)} %get-tuple-element.708, s32[]{:T(128)} %get-tuple-element.696), kind=kOutput, calls=%fused_computation.294.clone.1.clone | convolution fusion | flops 6596665344 | bytes 39355904 | tf_op jit(solution)/shard_map/while/body/eval_jaxpr/dot_general | solution.py:249
  424.3 6.7 select_reduce_fusion.3
  431.2 13.2 %all-gather = f32[4,1,1024]{2,1,0:T(1,128)S(1)} all-gather(f32[1,1,1024]{2,1,0:T(1,128)S(1)} %reshape.547), channel_id=1, replica_groups=mesh['dp'=8,'mp'=4] {'mp'}, dimensions={0}, use_global_device_ids=true | all-gather | bytes 20480 | tf_op jit(solution)/shard_map/all_gather | solution.py:24
  444.4 13.4 %all-gather.1 = f32[4,1,1024]{2,1,0:T(1,128)S(1)} all-gather(f32[1,1,1024]{2,1,0:T(1,128)S(1)} %reshape.549), channel_id=1, replica_groups=mesh['dp'=8,'mp'=4] {'mp'}, dimensions={0}, use_global_device_ids=true | all-gather | bytes 20480 | tf_op jit(solution)/shard_map/all_gather | solution.py:24
  457.8 13.2 %all-gather.2 = f32[4,1,1024]{2,1,0:T(1,128)S(1)} all-gather(f32[1,1,1024]{2,1,0:T(1,128)S(1)} %reshape.551), channel_id=1, replica_groups=mesh['dp'=8,'mp'=4] {'mp'}, dimensions={0}, use_global_device_ids=true | all-gather | bytes 20480 | tf_op jit(solution)/shard_map/all_gather | solution.py:24
  471.9 135.9 %while.55 = (s32[]{:T(128)}, f32[4,256,1024]{2,1,0:T(8,128)}, bf16[4,256,1024]{2,1,0:T(8,128)(2,1)}, bf16[1024,12576]{1,0:T(8,128)(2,1)}, f32[4,256]{1,0:T(4,128...) while((s32[]{:T(128)}, f32[4,256,1024]{2,1,0:T(8,128)}, ...), condition=%wide.region_21.22_spmd.clone.clone, body=%wide.region_20.21_spmd.clone.sunk.clone | while | flops 13206208512 | bytes 53487712 | solution.py:273
  471.9 34.0 %fusion.260 = f32[4,256,1024]{2,1,0:T(8,128)} fusion(f32[4,256,1024]{2,1,0:T(8,128)} %get-tuple-element.742, s32[]{:T(128)} %get-tuple-element.741, bf16[1024,12576]{1,0:T(8,128)(2,1)} %get-tuple-element.752, f32[256]{0:T(256)S(1)} %bitcast.331, s32[256]{0:T(256)S(1)} %bitcast.330, f32[256]{0:T(256)S(1)} %bitcast.332, ...), kind=kOutput, calls=%fused_computation.22.clone.1.clone | convolution fusion | flops 13206208512 | bytes 53481472 | tf_op jit(solution)/shard_map/while/body/eval_jaxpr/lv,dv->ld/dot_general | solution.py:271
  505.9 34.0 %fusion.260 = f32[4,256,1024]{2,1,0:T(8,128)} fusion(f32[4,256,1024]{2,1,0:T(8,128)} %get-tuple-element.742, s32[]{:T(128)} %get-tuple-element.741, bf16[1024,12576]{1,0:T(8,128)(2,1)} %get-tuple-element.752, f32[256]{0:T(256)S(1)} %bitcast.331, s32[256]{0:T(256)S(1)} %bitcast.330, f32[256]{0:T(256)S(1)} %bitcast.332, ...), kind=kOutput, calls=%fused_computation.22.clone.1.clone | convolution fusion | flops 13206208512 | bytes 53481472 | tf_op jit(solution)/shard_map/while/body/eval_jaxpr/lv,dv->ld/dot_general | solution.py:271
  539.9 33.9 %fusion.260 = f32[4,256,1024]{2,1,0:T(8,128)} fusion(f32[4,256,1024]{2,1,0:T(8,128)} %get-tuple-element.742, s32[]{:T(128)} %get-tuple-element.741, bf16[1024,12576]{1,0:T(8,128)(2,1)} %get-tuple-element.752, f32[256]{0:T(256)S(1)} %bitcast.331, s32[256]{0:T(256)S(1)} %bitcast.330, f32[256]{0:T(256)S(1)} %bitcast.332, ...), kind=kOutput, calls=%fused_computation.22.clone.1.clone | convolution fusion | flops 13206208512 | bytes 53481472 | tf_op jit(solution)/shard_map/while/body/eval_jaxpr/lv,dv->ld/dot_general | solution.py:271
  573.9 33.9 %fusion.260 = f32[4,256,1024]{2,1,0:T(8,128)} fusion(f32[4,256,1024]{2,1,0:T(8,128)} %get-tuple-element.742, s32[]{:T(128)} %get-tuple-element.741, bf16[1024,12576]{1,0:T(8,128)(2,1)} %get-tuple-element.752, f32[256]{0:T(256)S(1)} %bitcast.331, s32[256]{0:T(256)S(1)} %bitcast.330, f32[256]{0:T(256)S(1)} %bitcast.332, ...), kind=kOutput, calls=%fused_computation.22.clone.1.clone | convolution fusion | flops 13206208512 | bytes 53481472 | tf_op jit(solution)/shard_map/while/body/eval_jaxpr/lv,dv->ld/dot_general | solution.py:271
  608.5 153.3 %all-reduce.10.cloned.1.call-done = f32[1024,1024]{1,0:T(8,128)} async-done(((f32[1024,1024]{1,0:T(8,128)}), f32[1024,1024]{1,0:T(8,128)}) %all-reduce.10.cloned.1.call-update) | async-done | bytes 4194320 | tf_op jit(solution)/shard_map/psum | solution.py:282
  799.6 140.3 %reduce-scatter.2.cloned.1.call-done = f32[8,32,128]{2,1,0:T(8,128)} async-done(((f32[8,1024,128]{2,1,0:T(8,128)}), f32[8,32,128]{2,1,0:T(8,128)}) %reduce-scatter.2.cloned.1.call-update) | async-done | bytes 131088 | tf_op jit(solution)/shard_map/reduce_scatter | solution.py:333
  941.4 18.1 %psum.37 = f32[]{:T(128)} all-reduce(f32[]{:T(128)} %get-tuple-element.415), channel_id=1, replica_groups=mesh['dp'=8,'mp'=4] {'dp'}, use_global_device_ids=true, to_apply=%region_19.20 | all-reduce | flops 1 | bytes 8 | tf_op jit(solution)/shard_map/psum | solution.py:336
  959.5 44.9 %psum.39 = f32[]{:T(128)} all-reduce(f32[]{:T(128)} %multiply_reduce_fusion.4), channel_id=1, replica_groups=mesh['dp'=8,'mp'=4] {'dp','mp'}, use_global_device_ids=true, to_apply=%region_29.30 | all-reduce | flops 1 | bytes 8 | tf_op jit(solution)/shard_map/psum | solution.py:335
  (327 shorter events, 104.0 us)
Async XLA Ops:
  8.0 121.1 %copy-start = (bf16[1024,1024]{1,0:T(8,128)(2,1)S(1)}, bf16[1024,1024]{1,0:T(8,128)(2,1)}, u32[]{:S(2)}) copy-start(bf16[1024,1024]{1,0:T(8,128)(2,1)} %param.42) | copy-start | bytes 6291460
  8.0 112.2 %all-reduce.6.cloned.1.call-start = ((), (), s32[]{:S(2)}) async-start(), calls=%async_computation.1 | async-start | bytes 4194304 | tf_op jit(solution)/shard_map/psum | solution.py:185
  30.7 114.7 %all-gather.6.cloned.1.call-start = ((), (), s32[]{:S(2)}) async-start(), calls=%async_computation.2 | async-start | bytes 2162688 | tf_op jit(solution)/shard_map/all_gather | solution.py:171
  31.5 290.1 %all-reduce.8.cloned.1.call-start = ((), (), s32[]{:S(2)}) async-start(), calls=%async_computation.3 | async-start | bytes 8388608 | tf_op jit(solution)/shard_map/psum | solution.py:241
  31.7 294.2 %copy-start.57 = (f32[1,1024]{1,0:T(1,128)}, f32[1,1024]{1,0:T(1,128)S(1)}, u32[]{:S(2)}) copy-start(f32[1,1024]{1,0:T(1,128)S(1)} %get-tuple-element.447) | copy-start | bytes 12292
  31.9 119.4 %copy-start.45 = (f32[1024,8]{0,1:T(8,128)}, f32[1024,8]{0,1:T(8,128)S(1)}, u32[]{:S(2)}) copy-start(f32[1024,8]{0,1:T(8,128)S(1)} %get-tuple-element.452) | copy-start | bytes 98308
  31.9 119.4 %copy-start.47 = (f32[1024,8]{0,1:T(8,128)}, f32[1024,8]{0,1:T(8,128)S(1)}, u32[]{:S(2)}) copy-start(f32[1024,8]{0,1:T(8,128)S(1)} %get-tuple-element.453) | copy-start | bytes 98308
  147.0 14.4 %copy-start.44 = (bf16[1,1024,128]{2,1,0:T(8,128)(2,1)}, bf16[1,1024,128]{2,1,0:T(8,128)(2,1)S(1)}, u32[]{:S(2)}) copy-start(bf16[1,1024,128]{2,1,0:T(8,128)(2,1)S(1)} %get-tuple-element.423) | copy-start | bytes 786436
  151.3 9.3 copy-start.14
  167.9 8.1 copy-start.76
  167.9 153.6 %copy-start.4 = (bf16[1024,1024]{1,0:T(8,128)(2,1)S(1)}, bf16[1024,1024]{1,0:T(8,128)(2,1)}, u32[]{:S(2)}) copy-start(bf16[1024,1024]{1,0:T(8,128)(2,1)} %all-reduce.6.cloned.1.call-done) | copy-start | bytes 6291460
  168.0 160.3 %all-gather.8.cloned.1.call-start = ((), (), s32[]{:S(2)}) async-start(), calls=%async_computation.4 | async-start | bytes 29196288 | tf_op jit(solution)/shard_map/all_gather | solution.py:172
  173.8 588.1 %all-reduce.10.cloned.1.call-start = ((), (), s32[]{:S(2)}) async-start(), calls=%async_computation.5 | async-start | bytes 8388608 | tf_op jit(solution)/shard_map/psum | solution.py:282
  607.8 154.1 %copy-start.5 = (bf16[1024,1024]{1,0:T(8,128)(2,1)S(1)}, bf16[1024,1024]{1,0:T(8,128)(2,1)}, u32[]{:S(2)}) copy-start(bf16[1024,1024]{1,0:T(8,128)(2,1)} %all-reduce.6.cloned.1.call-done) | copy-start | bytes 6291460
  607.8 154.1 %copy-start.56 = (f32[1024]{0:T(1024)S(1)}, f32[1024]{0:T(1024)}, u32[]{:S(2)}) copy-start(f32[1024]{0:T(1024)} %copy-done.55) | copy-start | bytes 12292
  607.8 154.1 %copy-start.58 = (f32[1,1024]{1,0:T(1,128)S(1)}, f32[1,1024]{1,0:T(1,128)}, u32[]{:S(2)}) copy-start(f32[1,1024]{1,0:T(1,128)} %copy-done.57) | copy-start | bytes 12292
  607.8 332.0 %reduce-scatter.2.cloned.1.call-start = ((), (), s32[]{:S(2)}) async-start(), calls=%async_computation.6 | async-start | bytes 4325376 | tf_op jit(solution)/shard_map/reduce_scatter | solution.py:333
  608.5 158.0 %copy-start.62 = (f32[1024]{0:T(1024)S(1)}, f32[1024]{0:T(1024)}, u32[]{:S(2)}) copy-start(f32[1024]{0:T(1024)} %copy-done.61) | copy-start | bytes 12292
  608.5 158.0 %copy-start.60 = (f32[1024]{0:T(1024)S(1)}, f32[1024]{0:T(1024)}, u32[]{:S(2)}) copy-start(f32[1024]{0:T(1024)} %copy-done.59) | copy-start | bytes 12292
  798.0 207.2 %copy-start.23 = (f32[8,128,128]{2,1,0:T(8,128)S(1)}, f32[8,128,128]{2,1,0:T(8,128)}, u32[]{:S(2)}) copy-start(f32[8,128,128]{2,1,0:T(8,128)} %param.49) | copy-start | bytes 1572868
  798.0 207.2 %copy-start.53 = (f32[8,32,128]{2,1,0:T(8,128)S(1)}, f32[8,32,128]{2,1,0:T(8,128)}, u32[]{:S(2)}) copy-start(f32[8,32,128]{2,1,0:T(8,128)} %param.48) | copy-start | bytes 393220
  798.0 207.2 %copy-start.54 = (f32[8,32,128]{2,1,0:T(8,128)S(1)}, f32[8,32,128]{2,1,0:T(8,128)}, u32[]{:S(2)}) copy-start(f32[8,32,128]{2,1,0:T(8,128)} %param.47) | copy-start | bytes 393220
  798.0 208.7 %copy-start.43 = (f32[8,32,128]{2,1,0:T(8,128)S(1)}, f32[8,32,128]{2,1,0:T(8,128)}, u32[]{:S(2)}) copy-start(f32[8,32,128]{2,1,0:T(8,128)} %param.46) | copy-start | bytes 393220
  798.0 210.3 %copy-start.1 = (bf16[1024,1024]{1,0:T(8,128)(2,1)S(1)}, bf16[1024,1024]{1,0:T(8,128)(2,1)}, u32[]{:S(2)}) copy-start(bf16[1024,1024]{1,0:T(8,128)(2,1)} %param.42) | copy-start | bytes 6291460
  (62 other events, 168.4 us)
Sparse Core Ops, SparseCore 0:
  30.9 89.3 all-reduce.5
  168.0 153.4 all-reduce.7
  608.0 153.8 all-reduce.9
Sparse Core Ops, SparseCore 1:
  34.7 98.1 all-gather.5
  173.9 127.9 all-gather.7
  799.7 140.1 reduce-scatter.1
where the time goes:
time: 1020 us
  waiting for transfers between devices  524 us (51%)
  matrix products  271 us (27%)
  blocking collectives  103 us (10%)
  other arithmetic  61.3 us (6%)
  local copies, waits for them, and re-layouts  36.2 us (4%)
  between operations  20.9 us (2%)
    psum x1, waiting for transfers between devices, per_device(): lax.psum(head_grad, 'mp')  153 us
    psum x1, waiting for transfers between devices, per_device(): resid = start_rows + lax.psum(partial_value, 'mp')  142 us
    reduce_scatter x1, waiting for transfers between devices, per_device(): lax.psum_scatter(gradient, ('dp', 'mp'), scatter_dimension=1, tiled=True)  140 us
    dot_general x4, matrix products, block_back(): jnp.einsum('lv,dv->ld', logit_grad, head_local, preferred_element_type=jn...  136 us
    psum x1, waiting for transfers between devices, per_device(): start_rows = lax.psum(picked.astype(jnp.bfloat16), 'mp').astype(jnp.float32)  87.9 us
    dot_general x4, matrix products, block_stats(): logits = jnp.dot(rows_here, head_local, preferred_element_type=jnp.float32)  75.4 us
    psum x1, blocking collectives, per_device(): norm_squared = lax.psum(squares, ('dp', 'mp'))  44.9 us
    all_gather x3, blocking collectives, merged(): pieces = jax.tree.map(lambda part: lax.all_gather(part, axis), value)  39.8 us
  transfers between devices with their start and end apart: 6, of which 4 were waited for; matrix products, arithmetic and copies ran while one was open for 4% of the time, Pallas kernels for 0%

commit v1 on v0

--- a/solution.py
+++ b/solution.py
@@ -18,6 +18,12 @@
 BETA_SECOND = 0.999
 ADAM_EPS = 1e-08
 DECAY_RATE = 0.01
+
+
+def gather_and_add(value, name):
+    terms = lax.all_gather(value, name, axis=0, tiled=False)
+    total = terms.sum(axis=0)
+    return total
 
 
 def merged(value, axis, join):
@@ -238,7 +244,7 @@
         + jnp.einsum("lr,dr->ld", inner_out, adapters[7], preferred_element_type=jnp.float32)
         + jnp.dot(hidden, w_down, preferred_element_type=jnp.float32)
     )
-    resid = start_rows + lax.psum(partial_value, "mp")
+    resid = start_rows + gather_and_add(partial_value, "mp")
     final_rows = layer_norm(resid, ln_gain[2], ln_bias[2]).astype(jnp.bfloat16)
     row_block = min(256, rows)
     blocks = rows // row_block

time: 1020 us -> 1280 us (1.25)
  waiting for transfers between devices: 524 us -> 767 us
    all_gather x0 -> x1, waiting for transfers between devices: none -> 274 us  [gather_and_add(): terms = lax.all_gather(value, name, axis=0, tiled=False)]
    psum x1 -> x0, waiting for transfers between devices: 142 us -> none  [per_device(): resid = start_rows + lax.psum(partial_value, 'mp')]
    all_gather x1, waiting for transfers between devices: 0.01 us -> 112 us  [per_device(): head_local = lax.all_gather(unembed, 'dp', axis=0, tiled=True)]
  transfers between devices with their start and end apart: 6 -> 6, of which waited for: 4 -> 5; matrix products, arithmetic and copies ran while one was open for 4% -> 4% of each run, Pallas kernels for 0% -> 0%
where the time goes in v1:
time: 1280 us; the launch traced here: 1270 us
  waiting for transfers between devices  767 us (60%)
  matrix products  271 us (21%)
  blocking collectives  102 us (8%)
  other arithmetic  72.8 us (6%)
  local copies, waits for them, and re-layouts  36.4 us (3%)
  between operations  20.8 us (2%)
    all_gather x1, waiting for transfers between devices, gather_and_add(): terms = lax.all_gather(value, name, axis=0, tiled=False)  274 us
    psum x1, waiting for transfers between devices, per_device(): lax.psum(head_grad, 'mp')  153 us
    reduce_scatter x1, waiting for transfers between devices, per_device(): lax.psum_scatter(gradient, ('dp', 'mp'), scatter_dimension=1, tiled=True)  141 us
    dot_general x4, matrix products, block_back(): jnp.einsum('lv,dv->ld', logit_grad, head_local, preferred_element_type=jn...  136 us
    all_gather x1, waiting for transfers between devices, per_device(): head_local = lax.all_gather(unembed, 'dp', axis=0, tiled=True)  112 us
    psum x1, waiting for transfers between devices, per_device(): start_rows = lax.psum(picked.astype(jnp.bfloat16), 'mp').astype(jnp.float32)  87.9 us
    dot_general x4, matrix products, block_stats(): logits = jnp.dot(rows_here, head_local, preferred_element_type=jnp.float32)  75.4 us
    psum x1, blocking collectives, per_device(): norm_squared = lax.psum(squares, ('dp', 'mp'))  45 us
  transfers between devices with their start and end apart: 6, of which 5 were waited for; matrix products, arithmetic and copies ran while one was open for 4% of the time, Pallas kernels for 0%

profile of v1, /device:TPU:14, one launch (start us, length us, event | category | flops | bytes accessed | tf_op | source)
XLA Modules:
  0.0 1271.0 jit_solution(9383689643281692479)
XLA Ops:
  9.6 17.7 %gather_fusion = bf16[1024,1024]{1,0:T(8,128)(2,1)} fusion(bf16[12576,1024]{1,0:T(8,128)(2,1)} %param.37, s32[1024]{0:T(1024)S(1)} %broadcast_clamp_fusion), kind=kCustom, calls=%fused_computation | custom fusion | bytes 4198400 | tf_op jit(solution)/shard_map/gather | solution.py:189
  32.3 87.9 %all-reduce.5.cloned.1.call-done = bf16[1024,1024]{1,0:T(8,128)(2,1)} async-done(((bf16[1024,1024]{1,0:T(8,128)(2,1)}), bf16[1024,1024]{1,0:T(8,128)(2,1)}) %all-reduce.5.cloned.1.call-update) | async-done | bytes 2097168 | tf_op jit(solution)/shard_map/psum | solution.py:191
  129.1 16.5 %fusion.56 = f32[1024,1024]{1,0:T(8,128)} fusion(bf16[1024,1024]{1,0:T(8,128)(2,1)S(1)} %copy-done, f32[1024]{0:T(1024)S(1)} %copy-done.75, bf16[1024,1024]{1,0:T(8,128)(2,1)} %param.40, bf16[1024,1024]{1,0:T(8,128)(2,1)} %all-reduce.5.cloned.1.call-done, f32[1024]{0:T(1024)S(1)} %bitcast.340, f32[1024]{0:T(1024)S(1)} %bitcast.339, ...), kind=kOutput, calls=%fused_computation.95 | convolution fusion | flops 4370464768 | bytes 10506240 | tf_op jit(solution)/shard_map/dot_general | solution.py:245
  178.9 273.5 %all-gather.12.cloned.1.call-done = f32[4096,1024]{1,0:T(8,128)} async-done(((f32[1024,1024]{1,0:T(8,128)}), f32[4096,1024]{1,0:T(8,128)}) %all-gather.12.cloned.1.call-update) | async-done | bytes 16777232 | tf_op jit(solution)/shard_map/all_gather | solution.py:24
  452.5 10.8 reduce_sum.176
  471.2 111.7 %all-gather.10.cloned.1.call-done = bf16[1024,12576]{1,0:T(8,128)(2,1)} async-done(((bf16[128,12576]{1,0:T(8,128)(2,1)}), bf16[1024,12576]{1,0:T(8,128)(2,1)}) %all-gather.10.cloned.1.call-update) | async-done | bytes 25755664 | tf_op jit(solution)/shard_map/all_gather | solution.py:178
  582.9 103.0 %while.54 = (s32[]{:T(128)}, f32[4,256]{1,0:T(4,128)S(1)}, f32[4,256]{1,0:T(4,128)S(1)}, f32[4,256]{1,0:T(4,128)S(1)}, bf16[4,256,1024]{2,1,0:T(8,128)(2,1)}, /*...) while((s32[]{:T(128)}, f32[4,256]{1,0:T(4,128)S(1)}, ...), condition=%wide.region_14.15_spmd.clone.clone, body=%wide.region_10.14_spmd.clone.sunk.clone | while | flops 6612762112 | bytes 52246120 | solution.py:261
  583.1 18.8 %fusion.255 = (f32[256]{0:T(256)S(1)}, f32[256,12576]{0,1:T(8,128)}) fusion(bf16[1024,12576]{1,0:T(8,128)(2,1)} %get-tuple-element.709, bf16[4,256,1024]{2,1,0:T(8,128)(2,1)} %get-tuple-element.708, s32[]{:T(128)} %get-tuple-element.696), kind=kOutput, calls=%fused_computation.294.clone.1.clone | convolution fusion | flops 6596665344 | bytes 39355904 | tf_op jit(solution)/shard_map/while/body/eval_jaxpr/dot_general | solution.py:255
  601.9 6.7 select_reduce_fusion.3
  608.8 18.8 %fusion.255 = (f32[256]{0:T(256)S(1)}, f32[256,12576]{0,1:T(8,128)}) fusion(bf16[1024,12576]{1,0:T(8,128)(2,1)} %get-tuple-element.709, bf16[4,256,1024]{2,1,0:T(8,128)(2,1)} %get-tuple-element.708, s32[]{:T(128)} %get-tuple-element.696), kind=kOutput, calls=%fused_computation.294.clone.1.clone | convolution fusion | flops 6596665344 | bytes 39355904 | tf_op jit(solution)/shard_map/while/body/eval_jaxpr/dot_general | solution.py:255
  634.5 18.9 %fusion.255 = (f32[256]{0:T(256)S(1)}, f32[256,12576]{0,1:T(8,128)}) fusion(bf16[1024,12576]{1,0:T(8,128)(2,1)} %get-tuple-element.709, bf16[4,256,1024]{2,1,0:T(8,128)(2,1)} %get-tuple-element.708, s32[]{:T(128)} %get-tuple-element.696), kind=kOutput, calls=%fused_computation.294.clone.1.clone | convolution fusion | flops 6596665344 | bytes 39355904 | tf_op jit(solution)/shard_map/while/body/eval_jaxpr/dot_general | solution.py:255
  660.2 18.9 %fusion.255 = (f32[256]{0:T(256)S(1)}, f32[256,12576]{0,1:T(8,128)}) fusion(bf16[1024,12576]{1,0:T(8,128)(2,1)} %get-tuple-element.709, bf16[4,256,1024]{2,1,0:T(8,128)(2,1)} %get-tuple-element.708, s32[]{:T(128)} %get-tuple-element.696), kind=kOutput, calls=%fused_computation.294.clone.1.clone | convolution fusion | flops 6596665344 | bytes 39355904 | tf_op jit(solution)/shard_map/while/body/eval_jaxpr/dot_general | solution.py:255
  686.0 13.3 %all-gather.1 = f32[4,1,1024]{2,1,0:T(1,128)S(1)} all-gather(f32[1,1,1024]{2,1,0:T(1,128)S(1)} %reshape.548), channel_id=1, replica_groups=mesh['dp'=8,'mp'=4] {'mp'}, dimensions={0}, use_global_device_ids=true | all-gather | bytes 20480 | tf_op jit(solution)/shard_map/all_gather | solution.py:30
  699.2 13.2 %all-gather.2 = f32[4,1,1024]{2,1,0:T(1,128)S(1)} all-gather(f32[1,1,1024]{2,1,0:T(1,128)S(1)} %reshape.550), channel_id=1, replica_groups=mesh['dp'=8,'mp'=4] {'mp'}, dimensions={0}, use_global_device_ids=true | all-gather | bytes 20480 | tf_op jit(solution)/shard_map/all_gather | solution.py:30
  712.5 13.2 %all-gather.3 = f32[4,1,1024]{2,1,0:T(1,128)S(1)} all-gather(f32[1,1,1024]{2,1,0:T(1,128)S(1)} %reshape.552), channel_id=1, replica_groups=mesh['dp'=8,'mp'=4] {'mp'}, dimensions={0}, use_global_device_ids=true | all-gather | bytes 20480 | tf_op jit(solution)/shard_map/all_gather | solution.py:30
  726.6 135.8 %while.55 = (s32[]{:T(128)}, f32[4,256,1024]{2,1,0:T(8,128)}, bf16[4,256,1024]{2,1,0:T(8,128)(2,1)}, bf16[1024,12576]{1,0:T(8,128)(2,1)}, f32[4,256]{1,0:T(4,128...) while((s32[]{:T(128)}, f32[4,256,1024]{2,1,0:T(8,128)}, ...), condition=%wide.region_21.22_spmd.clone.clone, body=%wide.region_20.21_spmd.clone.sunk.clone | while | flops 13206208512 | bytes 53487712 | solution.py:279
  726.6 33.9 %fusion.260 = f32[4,256,1024]{2,1,0:T(8,128)} fusion(f32[4,256,1024]{2,1,0:T(8,128)} %get-tuple-element.742, s32[]{:T(128)} %get-tuple-element.741, bf16[1024,12576]{1,0:T(8,128)(2,1)} %get-tuple-element.752, f32[256]{0:T(256)S(1)} %bitcast.333, s32[256]{0:T(256)S(1)} %bitcast.332, f32[256]{0:T(256)S(1)} %bitcast.334, ...), kind=kOutput, calls=%fused_computation.22.clone.1.clone | convolution fusion | flops 13206208512 | bytes 53481472 | tf_op jit(solution)/shard_map/while/body/eval_jaxpr/lv,dv->ld/dot_general | solution.py:277
  760.6 33.9 %fusion.260 = f32[4,256,1024]{2,1,0:T(8,128)} fusion(f32[4,256,1024]{2,1,0:T(8,128)} %get-tuple-element.742, s32[]{:T(128)} %get-tuple-element.741, bf16[1024,12576]{1,0:T(8,128)(2,1)} %get-tuple-element.752, f32[256]{0:T(256)S(1)} %bitcast.333, s32[256]{0:T(256)S(1)} %bitcast.332, f32[256]{0:T(256)S(1)} %bitcast.334, ...), kind=kOutput, calls=%fused_computation.22.clone.1.clone | convolution fusion | flops 13206208512 | bytes 53481472 | tf_op jit(solution)/shard_map/while/body/eval_jaxpr/lv,dv->ld/dot_general | solution.py:277
  794.5 34.0 %fusion.260 = f32[4,256,1024]{2,1,0:T(8,128)} fusion(f32[4,256,1024]{2,1,0:T(8,128)} %get-tuple-element.742, s32[]{:T(128)} %get-tuple-element.741, bf16[1024,12576]{1,0:T(8,128)(2,1)} %get-tuple-element.752, f32[256]{0:T(256)S(1)} %bitcast.333, s32[256]{0:T(256)S(1)} %bitcast.332, f32[256]{0:T(256)S(1)} %bitcast.334, ...), kind=kOutput, calls=%fused_computation.22.clone.1.clone | convolution fusion | flops 13206208512 | bytes 53481472 | tf_op jit(solution)/shard_map/while/body/eval_jaxpr/lv,dv->ld/dot_general | solution.py:277
  828.5 33.9 %fusion.260 = f32[4,256,1024]{2,1,0:T(8,128)} fusion(f32[4,256,1024]{2,1,0:T(8,128)} %get-tuple-element.742, s32[]{:T(128)} %get-tuple-element.741, bf16[1024,12576]{1,0:T(8,128)(2,1)} %get-tuple-element.752, f32[256]{0:T(256)S(1)} %bitcast.333, s32[256]{0:T(256)S(1)} %bitcast.332, f32[256]{0:T(256)S(1)} %bitcast.334, ...), kind=kOutput, calls=%fused_computation.22.clone.1.clone | convolution fusion | flops 13206208512 | bytes 53481472 | tf_op jit(solution)/shard_map/while/body/eval_jaxpr/lv,dv->ld/dot_general | solution.py:277
  863.2 153.4 %all-reduce.7.cloned.1.call-done = f32[1024,1024]{1,0:T(8,128)} async-done(((f32[1024,1024]{1,0:T(8,128)}), f32[1024,1024]{1,0:T(8,128)}) %all-reduce.7.cloned.1.call-update) | async-done | bytes 4194320 | tf_op jit(solution)/shard_map/psum | solution.py:288
  1054.3 140.7 %reduce-scatter.2.cloned.1.call-done = f32[8,32,128]{2,1,0:T(8,128)} async-done(((f32[8,1024,128]{2,1,0:T(8,128)}), f32[8,32,128]{2,1,0:T(8,128)}) %reduce-scatter.2.cloned.1.call-update) | async-done | bytes 131088 | tf_op jit(solution)/shard_map/reduce_scatter | solution.py:339
  1196.5 17.0 %psum.29 = f32[]{:T(128)} all-reduce(f32[]{:T(128)} %get-tuple-element.415), channel_id=1, replica_groups=mesh['dp'=8,'mp'=4] {'dp'}, use_global_device_ids=true, to_apply=%region_19.20 | all-reduce | flops 1 | bytes 8 | tf_op jit(solution)/shard_map/psum | solution.py:342
  1213.5 45.0 %psum.31 = f32[]{:T(128)} all-reduce(f32[]{:T(128)} %multiply_reduce_fusion.4), channel_id=1, replica_groups=mesh['dp'=8,'mp'=4] {'dp','mp'}, use_global_device_ids=true, to_apply=%region_29.30 | all-reduce | flops 1 | bytes 8 | tf_op jit(solution)/shard_map/psum | solution.py:341
  (328 shorter events, 118.5 us)
Async XLA Ops:
  8.0 121.1 %copy-start = (bf16[1024,1024]{1,0:T(8,128)(2,1)S(1)}, bf16[1024,1024]{1,0:T(8,128)(2,1)}, u32[]{:S(2)}) copy-start(bf16[1024,1024]{1,0:T(8,128)(2,1)} %param.42) | copy-start | bytes 6291460
  8.0 112.2 %all-reduce.5.cloned.1.call-start = ((), (), s32[]{:S(2)}) async-start(), calls=%async_computation.1 | async-start | bytes 4194304 | tf_op jit(solution)/shard_map/psum | solution.py:191
  30.7 114.8 %all-gather.8.cloned.1.call-start = ((), (), s32[]{:S(2)}) async-start(), calls=%async_computation.2 | async-start | bytes 2162688 | tf_op jit(solution)/shard_map/all_gather | solution.py:177
  31.5 421.0 %all-gather.12.cloned.1.call-start = ((), (), s32[]{:S(2)}) async-start(), calls=%async_computation.6 | async-start | bytes 20971520 | tf_op jit(solution)/shard_map/all_gather | solution.py:24
  31.7 437.3 %copy-start.57 = (f32[1,1024]{1,0:T(1,128)}, f32[1,1024]{1,0:T(1,128)S(1)}, u32[]{:S(2)}) copy-start(f32[1,1024]{1,0:T(1,128)S(1)} %get-tuple-element.447) | copy-start | bytes 12292
  31.9 119.4 %copy-start.45 = (f32[1024,8]{0,1:T(8,128)}, f32[1024,8]{0,1:T(8,128)S(1)}, u32[]{:S(2)}) copy-start(f32[1024,8]{0,1:T(8,128)S(1)} %get-tuple-element.452) | copy-start | bytes 98308
  31.9 119.4 %copy-start.47 = (f32[1024,8]{0,1:T(8,128)}, f32[1024,8]{0,1:T(8,128)S(1)}, u32[]{:S(2)}) copy-start(f32[1024,8]{0,1:T(8,128)S(1)} %get-tuple-element.453) | copy-start | bytes 98308
  147.1 14.4 %copy-start.44 = (bf16[1,1024,128]{2,1,0:T(8,128)(2,1)}, bf16[1,1024,128]{2,1,0:T(8,128)(2,1)S(1)}, u32[]{:S(2)}) copy-start(bf16[1,1024,128]{2,1,0:T(8,128)(2,1)S(1)} %get-tuple-element.423) | copy-start | bytes 786436
  151.3 9.3 copy-start.14
  152.6 8.0 copy-start.8
  167.9 415.0 %all-gather.10.cloned.1.call-start = ((), (), s32[]{:S(2)}) async-start(), calls=%async_computation.3 | async-start | bytes 29196288 | tf_op jit(solution)/shard_map/all_gather | solution.py:178
  173.6 843.0 %all-reduce.7.cloned.1.call-start = ((), (), s32[]{:S(2)}) async-start(), calls=%async_computation.4 | async-start | bytes 8388608 | tf_op jit(solution)/shard_map/psum | solution.py:288
  452.5 10.8 copy-start.6
  862.4 154.1 %copy-start.7 = (bf16[1024,1024]{1,0:T(8,128)(2,1)S(1)}, bf16[1024,1024]{1,0:T(8,128)(2,1)}, u32[]{:S(2)}) copy-start(bf16[1024,1024]{1,0:T(8,128)(2,1)} %all-reduce.5.cloned.1.call-done) | copy-start | bytes 6291460
  862.4 154.1 %copy-start.56 = (f32[1024]{0:T(1024)S(1)}, f32[1024]{0:T(1024)}, u32[]{:S(2)}) copy-start(f32[1024]{0:T(1024)} %copy-done.55) | copy-start | bytes 12292
  862.4 154.1 %copy-start.58 = (f32[1,1024]{1,0:T(1,128)S(1)}, f32[1,1024]{1,0:T(1,128)}, u32[]{:S(2)}) copy-start(f32[1,1024]{1,0:T(1,128)} %copy-done.57) | copy-start | bytes 12292
  862.5 332.5 %reduce-scatter.2.cloned.1.call-start = ((), (), s32[]{:S(2)}) async-start(), calls=%async_computation.5 | async-start | bytes 4325376 | tf_op jit(solution)/shard_map/reduce_scatter | solution.py:339
  863.1 158.0 %copy-start.62 = (f32[1024]{0:T(1024)S(1)}, f32[1024]{0:T(1024)}, u32[]{:S(2)}) copy-start(f32[1024]{0:T(1024)} %copy-done.61) | copy-start | bytes 12292
  863.2 158.0 %copy-start.60 = (f32[1024]{0:T(1024)S(1)}, f32[1024]{0:T(1024)}, u32[]{:S(2)}) copy-start(f32[1024]{0:T(1024)} %copy-done.59) | copy-start | bytes 12292
  1052.7 206.5 %copy-start.23 = (f32[8,128,128]{2,1,0:T(8,128)S(1)}, f32[8,128,128]{2,1,0:T(8,128)}, u32[]{:S(2)}) copy-start(f32[8,128,128]{2,1,0:T(8,128)} %param.49) | copy-start | bytes 1572868
  1052.7 206.5 %copy-start.53 = (f32[8,32,128]{2,1,0:T(8,128)S(1)}, f32[8,32,128]{2,1,0:T(8,128)}, u32[]{:S(2)}) copy-start(f32[8,32,128]{2,1,0:T(8,128)} %param.48) | copy-start | bytes 393220
  1052.7 206.5 %copy-start.54 = (f32[8,32,128]{2,1,0:T(8,128)S(1)}, f32[8,32,128]{2,1,0:T(8,128)}, u32[]{:S(2)}) copy-start(f32[8,32,128]{2,1,0:T(8,128)} %param.47) | copy-start | bytes 393220
  1052.7 208.0 %copy-start.43 = (f32[8,32,128]{2,1,0:T(8,128)S(1)}, f32[8,32,128]{2,1,0:T(8,128)}, u32[]{:S(2)}) copy-start(f32[8,32,128]{2,1,0:T(8,128)} %param.46) | copy-start | bytes 393220
  1052.7 209.6 %copy-start.1 = (bf16[1024,1024]{1,0:T(8,128)(2,1)S(1)}, bf16[1024,1024]{1,0:T(8,128)(2,1)}, u32[]{:S(2)}) copy-start(bf16[1024,1024]{1,0:T(8,128)(2,1)} %param.42) | copy-start | bytes 6291460
  (62 other events, 169.1 us)
Sparse Core Ops, SparseCore 0:
  30.9 89.3 all-reduce.4
  168.0 284.4 all-gather.11
  454.3 128.5 all-gather.9
  862.6 153.8 all-reduce.6
Sparse Core Ops, SparseCore 1:
  34.7 98.1 all-gather.7
  1054.4 140.5 reduce-scatter.1
